TPU v7x, 128 devices: a whole 4x4x4 slice. The times are simulated.
128 devices in a mesh: seq: 8 (over z, core), tp: 16 (over x, y).
Axes of the slice: x: 4, y: 4, z: 4, core: 2. Of those that a mesh axis runs over, the one named last changes fastest.
Arguments:
- sequence_in: bfloat16 [1536, 4096], P('tp', 'seq')
- conv_weight: bfloat16 [3, 1536, 3, 1536], P(None, 'tp')
- norm_gain: float32 [3, 1536], P(None, 'tp'), may hold values from 0.1 to 1.9
- tissue_scale: float32 [367, 1536], replicated, may hold values from 0.3 to 3
- donor_offset: int32 [2048], P('seq'), may hold values from 0 to 511
- acceptor_owner: int32 [2048, 1], P('seq'), may hold values from 0 to 7; in each aligned block of 256 rows (0 to 255, 256 to 511, ...) at most 128 rows name the same one
- acceptor_offset: int32 [2048], P('seq'), may hold values from 0 to 511
- tissue: int32 [2048], P('seq'), may hold values from 0 to 366
- tower_grad: float32 [1536, 4096], P('tp', 'seq'), may hold values from -6 to 6
- score_grad: float32 [2048], P('seq'), may hold values from -24 to 24
Outputs:
- scores: float32 [2048], P('seq')
- input_grad: float32 [1536, 4096], P('tp', 'seq')
- weight_grad: float32 [3, 1536, 3, 1536], P(None, 'tp')
- gain_grad: float32 [3, 1536], P(None, 'tp')
Inputs may be any that keep to these rules, and one draw needn't show every extreme that they name: `acceptor_owner`: among the 256 junctions of one index of seq, at most 128 have their acceptor on one index of seq.
All inputs are finite; a program needn't handle non-finite values.
Results may differ from a plain program's by a relative error of at most 0.025.
Values may be sent and summed in bfloat16 or wider, within the bound.
A program may use at most 128 MiB of HBM per device.

v0:
```python
import math
import jax
import jax.numpy as jnp
from jax import lax
from jax.sharding import PartitionSpec as P

CHANNELS = 1536
LAYERS = 3
CAP = 128
EPSILON = 1e-06


def with_halo(x, sides, width):
    for axis, dim in sides:
        count, length = (lax.axis_size(axis), x.shape[dim])
        up = [(i, (i + 1) % count) for i in range(count - 1)]
        down = [(j, i) for i, j in up]
        last = lax.slice_in_dim(x, length - width, length, axis=dim)
        initial = lax.slice_in_dim(x, 0, width, axis=dim)
        before = lax.ppermute(last, axis, up)
        after = lax.ppermute(initial, axis, down)
        x = jnp.concatenate([before, x, after], axis=dim)
    return x


def gelu_fn(value):
    return jax.nn.gelu(value, approximate=True)


def widen(block, width):
    return with_halo(block, (("seq", 1),), width)


def forward_taps(weights, padded, reach, length):
    total = jnp.zeros((weights.shape[0], length), jnp.float32)
    for tap in range(3):
        total = total + jnp.dot(
            weights[:, tap, :],
            padded[:, tap * reach : tap * reach + length],
            preferred_element_type=jnp.float32,
        )
    return total


def backward_taps(weights, grad_pad, reach, length):
    total = jnp.zeros((weights.shape[2], length), jnp.float32)
    for tap in range(3):
        total = total + lax.dot_general(
            weights[:, tap, :],
            grad_pad[:, (2 - tap) * reach : (2 - tap) * reach + length],
            (((0,), (0,)), ((), ())),
            preferred_element_type=jnp.float32,
        )
    return total


def weight_taps(padded, grad_bf, reach, length):
    blocks = []
    for tap in range(3):
        blocks.append(
            lax.dot_general(
                grad_bf,
                padded[:, tap * reach : tap * reach + length],
                (((1,), (1,)), ((), ())),
                preferred_element_type=jnp.float32,
            )
        )
    return jnp.stack(blocks, axis=1)


def local(
    sequence_in,
    conv_weight,
    norm_gain,
    tissue_scale,
    donor_offset,
    acceptor_owner,
    acceptor_offset,
    tissue,
    tower_grad,
    score_grad,
):
    local_ch = sequence_in.shape[0]
    length = sequence_in.shape[1]
    seq_count = lax.axis_size("seq")
    state = sequence_in
    stored = []
    for layer in range(LAYERS):
        reach = 2 ** (layer + 3)
        stream = state.astype(jnp.float32)
        power = lax.psum(jnp.sum(stream * stream, axis=0), "tp") / CHANNELS
        inverse = 1.0 / jnp.sqrt(power + EPSILON)
        pre_act = stream * inverse[None, :] * norm_gain[layer][:, None]
        hidden = gelu_fn(pre_act).astype(jnp.bfloat16)
        padded = widen(hidden, reach)
        weights = conv_weight[layer]
        gathered = padded

        def fold_inputs(total, piece, start, weights=weights, reach=reach):
            return forward_taps(weights, piece, reach, length)

        mixed = fold_inputs(
            jnp.zeros((local_ch, length), jnp.float32),
            lax.all_gather(padded, "tp", axis=0, tiled=True),
            jnp.int32(0),
        )
        stored.append((state, inverse, pre_act, gathered))
        state = (stream + mixed).astype(jnp.bfloat16)
    owner = acceptor_owner[:, 0]
    member = (owner[:, None] == jnp.arange(seq_count, dtype=jnp.int32)[None, :]).astype(jnp.int32)
    slot = jnp.sum(jnp.cumsum(member, axis=0) * member, axis=1) - 1
    requests = jnp.zeros((seq_count, CAP), jnp.int32).at[owner, slot].set(acceptor_offset)
    rows_view = state.T
    offsets = lax.all_to_all(requests, "seq", split_axis=0, concat_axis=0, tiled=True)
    picked = rows_view[offsets]
    returned = lax.all_to_all(picked, "seq", split_axis=0, concat_axis=0, tiled=True)
    accept_cols = returned[owner, slot].astype(jnp.float32)
    donor_cols = rows_view[donor_offset].astype(jnp.float32)
    chan_start = lax.axis_index("tp") * local_ch
    local_table = lax.dynamic_slice_in_dim(tissue_scale, chan_start, local_ch, 1)
    tissue_hit = (
        tissue[:, None] == jnp.arange(tissue_scale.shape[0], dtype=jnp.int32)[None, :]
    ).astype(jnp.float32)
    tissue_rows = jnp.dot(tissue_hit, local_table, precision=lax.Precision.HIGHEST)
    root = math.sqrt(CHANNELS)
    partial_scores = jnp.sum(donor_cols * accept_cols * tissue_rows, axis=1) / root
    scores = lax.psum(partial_scores, "tp")
    weight_j = score_grad / root
    donor_back = weight_j[:, None] * accept_cols * tissue_rows
    accept_back = weight_j[:, None] * donor_cols * tissue_rows
    outgoing = jnp.zeros((seq_count, CAP, local_ch), jnp.float32).at[owner, slot].set(accept_back)
    incoming = lax.all_to_all(
        outgoing.astype(jnp.bfloat16), "seq", split_axis=0, concat_axis=0, tiled=True
    ).astype(outgoing.dtype)
    upstream = tower_grad.at[:, donor_offset].add(donor_back.T)
    upstream = upstream.at[:, offsets.reshape(-1)].add(incoming.reshape(-1, local_ch).T)
    weight_list = [None] * LAYERS
    gain_list = [None] * LAYERS
    for layer in reversed(range(LAYERS)):
        reach = 2 ** (layer + 3)
        old_state, inverse, pre_act, gathered = stored[layer]
        stream = old_state.astype(jnp.float32)
        grad_bf = upstream.astype(jnp.bfloat16)
        grad_pad = widen(grad_bf, reach)
        weights = conv_weight[layer]

        def term_rows(start, count, weights=weights, grad_pad=grad_pad, reach=reach):
            return backward_taps(weights, grad_pad, reach, length)

        back_hidden = lax.psum_scatter(
            term_rows(jnp.int32(0), local_ch * lax.axis_size("tp")).astype(jnp.bfloat16),
            "tp",
            scatter_dimension=0,
            tiled=True,
        ).astype(jnp.float32)

        def fold_weights(total, piece, start, grad_bf=grad_bf, reach=reach):
            return weight_taps(piece, grad_bf, reach, length)

        weight_term = fold_weights(
            jnp.zeros((local_ch, 3, CHANNELS), jnp.float32),
            lax.all_gather(gathered, "tp", axis=0, tiled=True),
            jnp.int32(0),
        )
        weight_list[layer] = lax.psum(weight_term.astype(jnp.bfloat16), "seq").astype(jnp.float32)
        _, gelu_back = jax.vjp(gelu_fn, pre_act)
        back_pre = gelu_back(back_hidden)[0]
        gain_list[layer] = jnp.sum(back_pre * stream * inverse[None, :], axis=1)
        back_norm = back_pre * norm_gain[layer][:, None]
        inner = lax.psum(jnp.sum(back_norm * stream, axis=0), "tp")
        upstream = (
            upstream
            + inverse[None, :] * back_norm
            - stream * (inverse**3)[None, :] * inner[None, :] / CHANNELS
        )
    gain_grad = lax.psum(jnp.stack(gain_list), "seq")
    return (scores, upstream, jnp.stack(weight_list), gain_grad)


def solution(mesh):
    return jax.shard_map(
        local,
        mesh=mesh,
        in_specs=(
            P("tp", "seq"),
            P(None, "tp", None, None),
            P(None, "tp"),
            P(),
            P("seq"),
            P("seq", None),
            P("seq"),
            P("seq"),
            P("tp", "seq"),
            P("seq"),
        ),
        out_specs=(P("seq"), P("tp", "seq"), P(None, "tp", None, None), P(None, "tp")),
        check_vma=False,
    )
```

profile of v0, /device:TPU:0, one launch (start us, length us, event | category | flops | bytes accessed | tf_op | source)
XLA Modules:
  0.0 813.4 jit_solution(14602728577334916671)
XLA Ops:
  7.2 1.4 slice_bitcast_fusion.30
  9.6 40.8 %psum.77 = f32[512]{0:T(512)S(1)} all-reduce(f32[512]{0:T(512)S(1)} %fusion.133), channel_id=1, replica_groups=mesh['seq'=8,'tp'=16] {'tp'}, use_global_device_ids=true, to_apply=%region_1.0 | all-reduce | flops 512 | bytes 4096 | tf_op jit(solution)/shard_map/psum | solution.py:91
  52.1 1.3 collective-permute-start
  53.4 1.3 collective-permute-start.1
  54.7 3.9 collective-permute-done.1
  59.5 3.2 slice_bitcast_fusion
  62.6 40.5 %all-gather.4.cloned.1.call-done = bf16[1536,528]{1,0:T(8,128)(2,1)} async-done(((bf16[96,528]{1,0:T(8,128)(2,1)}), bf16[1536,528]{1,0:T(8,128)(2,1)}) %all-gather.4.cloned.1.call-update) | async-done | bytes 1622032 | tf_op jit(solution)/shard_map/all_gather | solution.py:104
  103.1 2.4 fusion.37
  105.6 2.2 fusion.40
  108.2 38.1 %psum.78 = f32[512]{0:T(512)S(1)} all-reduce(f32[512]{0:T(512)S(1)} %get-tuple-element.50), channel_id=1, replica_groups=mesh['seq'=8,'tp'=16] {'tp'}, use_global_device_ids=true, to_apply=%region_3.0 | all-reduce | flops 512 | bytes 4096 | tf_op jit(solution)/shard_map/psum | solution.py:91
  147.1 1.3 collective-permute-start.2
  148.4 1.3 collective-permute-start.3
  149.7 3.6 collective-permute-done.3
  154.1 42.9 %all-gather.6.cloned.1.call-done = bf16[1536,544]{1,0:T(8,128)(2,1)} async-done(((bf16[96,544]{1,0:T(8,128)(2,1)}), bf16[1536,544]{1,0:T(8,128)(2,1)}) %all-gather.6.cloned.1.call-update) | async-done | bytes 1671184 | tf_op jit(solution)/shard_map/all_gather | solution.py:104
  197.1 2.3 fusion.28
  200.5 38.3 %psum.79 = f32[512]{0:T(512)S(1)} all-reduce(f32[512]{0:T(512)S(1)} %get-tuple-element.52), channel_id=1, replica_groups=mesh['seq'=8,'tp'=16] {'tp'}, use_global_device_ids=true, to_apply=%region_5.0 | all-reduce | flops 512 | bytes 4096 | tf_op jit(solution)/shard_map/psum | solution.py:91
  240.3 1.3 collective-permute-start.4
  241.6 1.3 collective-permute-start.5
  242.9 3.6 collective-permute-done.5
  248.8 38.6 %scatter_fusion = s32[8,128]{1,0:T(8,128)} fusion(s32[8,128]{1,0:T(8,128)} %broadcast.150, s32[256]{0:T(256)S(1)} %bitcast.150, s32[256]{0:T(256)} %param.16), kind=kCustom, calls=%fused_computation.3 | custom fusion | bytes 5120 | tf_op jit(solution)/shard_map/scatter | solution.py:112
  287.5 6.3 all-to-all-start
  294.4 4.6 all-to-all-done
  299.1 2.4 fusion.19
  301.5 2.2 fusion.22
  304.2 3.2 gather_fusion.1
  308.3 3.4 all-to-all-start.1
  312.7 5.7 all-to-all-done.1
  318.6 1.7 gather_fusion.2
  322.2 16.8 %scatter_fusion.2 = f32[8,128,96]{2,1,0:T(8,128)S(1)} fusion(f32[8,128,96]{2,1,0:T(8,128)S(1)} %broadcast_in_dim.5, s32[256]{0:T(256)S(1)} %bitcast.151, f32[256,96]{1,0:T(8,128)} %copy.100), kind=kCustom, calls=%fused_computation.5 | custom fusion | bytes 296960 | tf_op jit(solution)/shard_map/scatter | solution.py:131
  339.8 4.0 all-to-all-start.2
  344.0 2.4 scatter_fusion.1
  346.4 4.3 all-to-all-done.2
  351.7 6.3 scatter_fusion.3
  358.1 2.7 collective-permute-start.7
  360.8 1.6 fusion.104
  362.4 1.3 collective-permute-start.6
  364.3 1.7 collective-permute-done.6
  366.0 1.8 fusion.6
  368.0 71.8 %reduce-scatter.4.cloned.1.call-done = bf16[96,512]{1,0:T(8,128)(2,1)} async-done(((bf16[1536,512]{1,0:T(8,128)(2,1)}), bf16[96,512]{1,0:T(8,128)(2,1)}) %reduce-scatter.4.cloned.1.call-update) | async-done | bytes 98320 | tf_op jit(solution)/shard_map/reduce_scatter | solution.py:150
  439.8 1.3 multiply_reduce_fusion
  441.0 38.1 %psum.81 = f32[512]{0:T(512)S(1)} all-reduce(f32[512]{0:T(512)S(1)} %get-tuple-element.7), channel_id=1, replica_groups=mesh['seq'=8,'tp'=16] {'tp'}, use_global_device_ids=true, to_apply=%region_17.18 | all-reduce | flops 512 | bytes 4096 | tf_op jit(solution)/shard_map/psum | solution.py:170
  479.2 1.8 fusion.168
  481.1 1.4 collective-permute-start.9
  482.5 1.6 fusion.102
  484.1 1.3 collective-permute-start.8
  486.1 2.9 collective-permute-done.8
  488.9 1.8 fusion.7
  490.9 2.6 fusion.16
  499.2 64.4 %reduce-scatter.6.cloned.1.call-done = bf16[96,512]{1,0:T(8,128)(2,1)} async-done(((bf16[1536,512]{1,0:T(8,128)(2,1)}), bf16[96,512]{1,0:T(8,128)(2,1)}) %reduce-scatter.6.cloned.1.call-update) | async-done | bytes 98320 | tf_op jit(solution)/shard_map/reduce_scatter | solution.py:150
  563.7 1.3 multiply_reduce_fusion.1
  564.9 38.3 %psum.82 = f32[512]{0:T(512)S(1)} all-reduce(f32[512]{0:T(512)S(1)} %get-tuple-element.5), channel_id=1, replica_groups=mesh['seq'=8,'tp'=16] {'tp'}, use_global_device_ids=true, to_apply=%region_20.21 | all-reduce | flops 512 | bytes 4096 | tf_op jit(solution)/shard_map/psum | solution.py:170
  603.3 1.3 fusion.167
  604.6 2.3 fusion.10
  609.5 1.3 collective-permute-start.11
  611.4 1.3 collective-permute-start.10
  613.4 2.9 collective-permute-done.10
  616.3 1.8 fusion.8
  618.1 55.7 %all-reduce.4.cloned.1.call-done = (bf16[1,96,3,1536]{3,1,2,0:T(8,128)(2,1)}, bf16[1,96,3,1536]{3,1,2,0:T(8,128)(2,1)}, bf16[1,96,3,1536]{3,1,2,0:T(8,128)(2,1)}) async-done(((bf16[1,96,3,1536]{3,1,2,0:T(8,128)(2,1)}, bf16[1,96,3,1536]{3,1,2,0:T(8,128)(2,1)}, bf16[1,96,3,1536]{3,1,2,0:T(8,128)(2,1)}), (bf16[1,96,3,1536]{3,1,2,0:T(8,128)(2,1)}, bf16[1,96,3,1536]{3,1,2,0:T(8,128)(2,1)}, ...) | async-done | bytes 2654224 | tf_op jit(solution)/shard_map/psum | solution.py:165
  673.8 4.5 maximum_convert_fusion
  678.3 72.7 %reduce-scatter.8.cloned.1.call-done = bf16[96,512]{1,0:T(8,128)(2,1)} async-done(((bf16[1536,512]{1,0:T(8,128)(2,1)}), bf16[96,512]{1,0:T(8,128)(2,1)}) %reduce-scatter.8.cloned.1.call-update) | async-done | bytes 98320 | tf_op jit(solution)/shard_map/reduce_scatter | solution.py:150
  751.1 1.3 fusion.142
  752.3 13.7 %psum.87 = f32[3,96]{1,0:T(4,128)} all-reduce(f32[3,96]{1,0:T(4,128)S(1)} %pad_maximum_fusion.15), channel_id=1, replica_groups=mesh['seq'=8,'tp'=16] {'seq'}, use_global_device_ids=true, to_apply=%region_30.31 | all-reduce | flops 288 | bytes 2304 | tf_op jit(solution)/shard_map/psum | solution.py:176
  766.1 38.6 %all-reduce = (f32[256]{0:T(256)}, f32[512]{0:T(512)S(1)}) all-reduce(f32[256]{0:T(256)S(1)} %broadcast_multiply_fusion.1, f32[512]{0:T(512)S(1)} %get-tuple-element.9), channel_id=1, replica_groups=mesh['seq'=8,'tp'=16] {'tp'}, use_global_device_ids=true, to_apply=%region_11.12 | all-reduce | flops 768 | bytes 6144 | tf_op jit(solution)/shard_map/psum | solution.py:127
  804.7 1.8 fusion.139
  (152 shorter events, 28.7 us)
Async XLA Ops:
  7.2 313.2 %copy-start = (f32[367,1536]{1,0:T(8,128)S(1)}, f32[367,1536]{1,0:T(8,128)}, u32[]{:S(2)}) copy-start(f32[367,1536]{1,0:T(8,128)} %param.13) | copy-start | bytes 6764548
  7.2 96.0 %all-gather.4.cloned.1.call-start = ((), (), s32[]{:S(2)}) async-start(), calls=%async_computation.6 | async-start | bytes 2088960 | tf_op jit(solution)/shard_map/all_gather | solution.py:104
  8.7 54.0 %copy-start.22 = (f32[96]{0:T(128)}, f32[96]{0:T(128)S(1)}, u32[]{:S(2)}) copy-start(f32[96]{0:T(128)S(1)} %get-tuple-element.46) | copy-start | bytes 1156
  8.7 138.3 %copy-start.24 = (f32[96]{0:T(128)}, f32[96]{0:T(128)S(1)}, u32[]{:S(2)}) copy-start(f32[96]{0:T(128)S(1)} %get-tuple-element.47) | copy-start | bytes 1156
  52.1 2.6 collective-permute-start
  53.4 5.2 collective-permute-start.1
  59.4 137.7 %all-gather.6.cloned.1.call-start = ((), (), s32[]{:S(2)}) async-start(), calls=%async_computation.7 | async-start | bytes 2088960 | tf_op jit(solution)/shard_map/all_gather | solution.py:104
  62.6 137.5 %copy-start.1 = (bf16[96,3,1536]{2,0,1:T(8,128)(2,1)}, bf16[96,3,1536]{2,0,1:T(8,128)(2,1)S(1)}, u32[]{:S(2)}) copy-start(bf16[96,3,1536]{2,0,1:T(8,128)(2,1)S(1)} %get-tuple-element.23) | copy-start | bytes 2654212
  103.1 2.4 copy-start.5
  103.1 4.6 copy-start.7
  103.1 4.6 copy-start.31
  147.1 2.6 collective-permute-start.2
  148.4 4.9 collective-permute-start.3
  154.1 145.0 %all-gather.8.cloned.1.call-start = ((), (), s32[]{:S(2)}) async-start(), calls=%async_computation.8 | async-start | bytes 2088960 | tf_op jit(solution)/shard_map/all_gather | solution.py:104
  197.1 2.3 copy-start.9
  200.1 47.2 %copy-start.18 = (s32[256,1]{0,1:T(1,128)S(1)}, s32[256,1]{0,1:T(1,128)}, u32[]{:S(2)}) copy-start(s32[256,1]{0,1:T(1,128)} %param.15) | copy-start | bytes 3076
  200.5 93.3 %copy-start.29 = (s32[256]{0:T(256)S(1)}, s32[256]{0:T(256)}, u32[]{:S(2)}) copy-start(s32[256]{0:T(256)} %param.14) | copy-start | bytes 3076
  200.5 93.8 %copy-start.14 = (f32[96,512]{1,0:T(8,128)S(1)}, f32[96,512]{1,0:T(8,128)}, u32[]{:S(2)}) copy-start(f32[96,512]{1,0:T(8,128)} %param.18) | copy-start | bytes 589828
  239.4 7.8 copy-start.15
  240.3 2.6 collective-permute-start.4
  241.6 4.9 collective-permute-start.5
  287.5 11.6 %all-to-all-start = ((s32[8,1,128]{2,1,0:T(1,128)}), s32[8,1,128]{2,1,0:T(1,128)S(1)}, u32[]{:S(2)}, u32[]{:S(2)}) async-start(s32[8,1,128]{2,1,0:T(1,128)} %bitcast.27), calls=%async_computation | async-start | bytes 8192 | tf_op jit(solution)/shard_map/all_to_all | solution.py:114
  293.8 0.5 copy-start.17
  299.1 2.4 copy-start.3
  299.1 4.6 copy-start.11
  304.1 7.6 copy-start.30
  307.5 12.9 %copy-start.28 = (s32[256]{0:T(256)S(1)}, s32[256]{0:T(256)}, u32[]{:S(2)}) copy-start(s32[256]{0:T(256)} %param.17) | copy-start | bytes 3076
  308.3 10.1 %all-to-all-start.1 = ((bf16[8,128,96]{1,2,0:T(8,128)(2,1)}), bf16[8,128,96]{1,2,0:T(8,128)(2,1)S(1)}, u32[]{:S(2)}, u32[]{:S(2)}) async-start(bf16[8,128,96]{1,2,0:T(8,128)(2,1)} %copy.95), calls=%async_computation.1 | async-start | bytes 393216 | tf_op jit(solution)/shard_map/all_to_all | solution.py:116
  339.8 10.8 %all-to-all-start.2 = ((bf16[8,128,96]{1,2,0:T(8,128)(2,1)}), bf16[8,128,96]{1,2,0:T(8,128)(2,1)}, u32[]{:S(2)}, u32[]{:S(2)}) async-start(bf16[8,128,96]{1,2,0:T(8,128)(2,1)} %copy.101), calls=%async_computation.2 | async-start | bytes 393216 | tf_op jit(solution)/shard_map/all_to_all | solution.py:132
  343.9 95.9 %reduce-scatter.4.cloned.1.call-start = ((), (), s32[]{:S(2)}) async-start(), calls=%async_computation.9 | async-start | bytes 1671168 | tf_op jit(solution)/shard_map/reduce_scatter | solution.py:150
  358.1 5.6 copy-start.4
  358.1 5.6 collective-permute-start.7
  362.4 3.6 collective-permute-start.6
  367.8 72.0 %copy-start.16 = (f32[512]{0:T(512)S(1)}, f32[512]{0:T(512)}, u32[]{:S(2)}) copy-start(f32[512]{0:T(512)} %copy-done.15) | copy-start | bytes 6148
  367.8 72.0 %copy-start.26 = (f32[96]{0:T(128)S(1)}, f32[96]{0:T(128)}, u32[]{:S(2)}) copy-start(f32[96]{0:T(128)} %get-tuple-element.45) | copy-start | bytes 1156
  367.8 111.4 %copy-start.21 = (f32[512]{0:T(512)S(1)}, f32[512]{0:T(512)}, u32[]{:S(2)}) copy-start(f32[512]{0:T(512)} %get-tuple-element.43) | copy-start | bytes 6148
  367.8 195.9 %reduce-scatter.6.cloned.1.call-start = ((), (), s32[]{:S(2)}) async-start(), calls=%async_computation.10 | async-start | bytes 1671168 | tf_op jit(solution)/shard_map/reduce_scatter | solution.py:150
  481.0 4.4 copy-start.2
  481.1 4.3 collective-permute-start.9
  484.1 4.9 collective-permute-start.8
  490.8 183.0 %all-reduce.4.cloned.1.call-start = ((), (), s32[]{:S(2)}) async-start(), calls=%async_computation.12 | async-start | bytes 5308416 | tf_op jit(solution)/shard_map/psum | solution.py:165
  490.8 2.6 copy-start.12
  494.1 1.9 copy-start.10
  497.4 66.3 %copy-start.25 = (f32[96]{0:T(128)S(1)}, f32[96]{0:T(128)}, u32[]{:S(2)}) copy-start(f32[96]{0:T(128)} %copy-done.24) | copy-start | bytes 1156
  497.4 105.9 %copy-start.13 = (f32[96,512]{1,0:T(8,128)S(1)}, f32[96,512]{1,0:T(8,128)}, u32[]{:S(2)}) copy-start(f32[96,512]{1,0:T(8,128)} %get-tuple-element.18) | copy-start | bytes 589828
  497.4 105.9 %copy-start.20 = (f32[512]{0:T(512)S(1)}, f32[512]{0:T(512)}, u32[]{:S(2)}) copy-start(f32[512]{0:T(512)} %get-tuple-element.41) | copy-start | bytes 6148
  603.3 3.6 copy-start.32
  608.3 2.5 copy-start.6
  609.3 141.7 %reduce-scatter.8.cloned.1.call-start = ((), (), s32[]{:S(2)}) async-start(), calls=%async_computation.11 | async-start | bytes 1671168 | tf_op jit(solution)/shard_map/reduce_scatter | solution.py:150
  609.5 3.2 collective-permute-start.11
  611.4 4.9 collective-permute-start.10
  613.4 4.8 copy-start.27
  673.8 77.3 %copy-start.8 = (bf16[96,512]{1,0:T(8,128)(2,1)S(1)}, bf16[96,512]{1,0:T(8,128)(2,1)}, u32[]{:S(2)}) copy-start(bf16[96,512]{1,0:T(8,128)(2,1)} %param.10) | copy-start | bytes 294916
  673.8 77.3 %copy-start.23 = (f32[96]{0:T(128)S(1)}, f32[96]{0:T(128)}, u32[]{:S(2)}) copy-start(f32[96]{0:T(128)} %copy-done.22) | copy-start | bytes 1156
  673.8 130.9 %copy-start.19 = (f32[512]{0:T(512)S(1)}, f32[512]{0:T(512)}, u32[]{:S(2)}) copy-start(f32[512]{0:T(512)} %get-tuple-element.39) | copy-start | bytes 6148
Sparse Core Ops, SparseCore 0:
  59.5 43.5 all-gather.3
  154.2 42.8 all-gather.5
  247.4 42.8 all-gather.7
  367.9 71.7 reduce-scatter.3
  490.9 72.7 reduce-scatter.5
  609.5 64.2 all-reduce.3
  677.0 73.9 reduce-scatter.7
where the time goes:
time: 816 us; the launch traced here: 813 us
  waiting for transfers between devices  381 us (47%)
  blocking collectives  246 us (30%)
  local copies, waits for them, and re-layouts  71.9 us (9%)
  matrix products  35.4 us (4%)
  other arithmetic  32.8 us (4%)
  starting transfers between devices  30.9 us (4%)
  between operations  14.9 us (2%)
    reduce_scatter x3, waiting for transfers between devices, local(): lax.psum_scatter(term_rows(jnp.int32(0), local_ch * lax.axis_size('tp'))....  209 us
    psum x3, blocking collectives, local(): power = lax.psum(jnp.sum(stream * stream, axis=0), 'tp') / CHANNELS  117 us
    all_gather x3, waiting for transfers between devices, local(): lax.all_gather(padded, 'tp', axis=0, tiled=True)  83.4 us
    psum x2, blocking collectives, local(): inner = lax.psum(jnp.sum(back_norm * stream, axis=0), 'tp')  76.5 us
    psum x1, waiting for transfers between devices, local(): lax.psum(weight_term.astype(jnp.bfloat16), 'seq').astype(jnp.float32)  55.7 us
    psum x1, blocking collectives, local(): scores = lax.psum(partial_scores, 'tp')  38.6 us
    scatter x1, local copies, waits for them, and re-layouts, local(): jnp.zeros((seq_count, CAP), jnp.int32).at[owner, slot].set(acceptor_offset)  38.6 us
    ppermute x6, waiting for transfers between devices, with_halo(): after = lax.ppermute(initial, axis, down)  18.6 us
  transfers between devices with their start and end apart: 22, of which 15 were waited for; matrix products, arithmetic and copies ran while one was open for 8% of the time, Pallas kernels for 0%

commit v1 on v0

--- a/solution.py
+++ b/solution.py
@@ -124,7 +124,7 @@
     tissue_rows = jnp.dot(tissue_hit, local_table, precision=lax.Precision.HIGHEST)
     root = math.sqrt(CHANNELS)
     partial_scores = jnp.sum(donor_cols * accept_cols * tissue_rows, axis=1) / root
-    scores = lax.psum(partial_scores, "tp")
+    scores = jnp.sum(lax.all_gather(partial_scores, "tp"), axis=0)
     weight_j = score_grad / root
     donor_back = weight_j[:, None] * accept_cols * tissue_rows
     accept_back = weight_j[:, None] * donor_cols * tissue_rows

time: 816 us -> 817 us (level)
  waiting for transfers between devices: 381 us -> 361 us
  blocking collectives: 246 us -> 265 us
    psum x1 -> x0, blocking collectives: 38.6 us -> none  [local(): scores = lax.psum(partial_scores, 'tp')]
    psum x2 -> x3, blocking collectives: 76.5 us -> 115 us  [local(): inner = lax.psum(jnp.sum(back_norm * stream, axis=0), 'tp')]
    psum x1, waiting for transfers between devices: 55.7 us -> 35.1 us  [local(): lax.psum(weight_term.astype(jnp.bfloat16), 'seq').astype(jnp.float32)]
    all_gather x0 -> x1, blocking collectives: none -> 20.1 us  [local(): scores = jnp.sum(lax.all_gather(partial_scores, 'tp'), axis=0)]
where the time goes in v1:
time: 817 us; the launch traced here: 814 us
  waiting for transfers between devices  361 us (44%)
  blocking collectives  265 us (32%)
  local copies, waits for them, and re-layouts  71.1 us (9%)
  matrix products  35.4 us (4%)
  other arithmetic  34.6 us (4%)
  starting transfers between devices  30.9 us (4%)
  between operations  15 us (2%)
    reduce_scatter x3, waiting for transfers between devices, local(): lax.psum_scatter(term_rows(jnp.int32(0), local_ch * lax.axis_size('tp'))....  209 us
    psum x3, blocking collectives, local(): power = lax.psum(jnp.sum(stream * stream, axis=0), 'tp') / CHANNELS  117 us
    psum x3, blocking collectives, local(): inner = lax.psum(jnp.sum(back_norm * stream, axis=0), 'tp')  115 us
    all_gather x3, waiting for transfers between devices, local(): lax.all_gather(padded, 'tp', axis=0, tiled=True)  83.4 us
    scatter x1, local copies, waits for them, and re-layouts, local(): jnp.zeros((seq_count, CAP), jnp.int32).at[owner, slot].set(acceptor_offset)  38.4 us
    psum x1, waiting for transfers between devices, local(): lax.psum(weight_term.astype(jnp.bfloat16), 'seq').astype(jnp.float32)  35.1 us
    all_gather x1, blocking collectives, local(): scores = jnp.sum(lax.all_gather(partial_scores, 'tp'), axis=0)  20.1 us
    ppermute x6, waiting for transfers between devices, with_halo(): after = lax.ppermute(initial, axis, down)  18.6 us
  transfers between devices with their start and end apart: 22, of which 15 were waited for; matrix products, arithmetic and copies ran while one was open for 8% of the time, Pallas kernels for 0%

profile of v1, /device:TPU:0, one launch (start us, length us, event | category | flops | bytes accessed | tf_op | source)
XLA Modules:
  0.0 813.8 jit_solution(3684337275662829531)
XLA Ops:
  7.2 1.4 slice_bitcast_fusion.30
  9.6 40.8 %psum.70 = f32[512]{0:T(512)S(1)} all-reduce(f32[512]{0:T(512)S(1)} %fusion.133), channel_id=1, replica_groups=mesh['seq'=8,'tp'=16] {'tp'}, use_global_device_ids=true, to_apply=%region_1.0 | all-reduce | flops 512 | bytes 4096 | tf_op jit(solution)/shard_map/psum | solution.py:91
  52.1 1.3 collective-permute-start
  53.4 1.3 collective-permute-start.1
  54.7 3.9 collective-permute-done.1
  59.5 3.2 slice_bitcast_fusion
  62.6 40.5 %all-gather.6.cloned.1.call-done = bf16[1536,528]{1,0:T(8,128)(2,1)} async-done(((bf16[96,528]{1,0:T(8,128)(2,1)}), bf16[1536,528]{1,0:T(8,128)(2,1)}) %all-gather.6.cloned.1.call-update) | async-done | bytes 1622032 | tf_op jit(solution)/shard_map/all_gather | solution.py:104
  103.1 2.4 fusion.37
  105.6 2.2 fusion.40
  108.2 38.1 %psum.71 = f32[512]{0:T(512)S(1)} all-reduce(f32[512]{0:T(512)S(1)} %get-tuple-element.48), channel_id=1, replica_groups=mesh['seq'=8,'tp'=16] {'tp'}, use_global_device_ids=true, to_apply=%region_3.0 | all-reduce | flops 512 | bytes 4096 | tf_op jit(solution)/shard_map/psum | solution.py:91
  147.1 1.3 collective-permute-start.2
  148.4 1.3 collective-permute-start.3
  149.7 3.6 collective-permute-done.3
  154.1 42.9 %all-gather.8.cloned.1.call-done = bf16[1536,544]{1,0:T(8,128)(2,1)} async-done(((bf16[96,544]{1,0:T(8,128)(2,1)}), bf16[1536,544]{1,0:T(8,128)(2,1)}) %all-gather.8.cloned.1.call-update) | async-done | bytes 1671184 | tf_op jit(solution)/shard_map/all_gather | solution.py:104
  197.1 2.3 fusion.28
  200.5 38.3 %psum.72 = f32[512]{0:T(512)S(1)} all-reduce(f32[512]{0:T(512)S(1)} %get-tuple-element.50), channel_id=1, replica_groups=mesh['seq'=8,'tp'=16] {'tp'}, use_global_device_ids=true, to_apply=%region_5.0 | all-reduce | flops 512 | bytes 4096 | tf_op jit(solution)/shard_map/psum | solution.py:91
  240.3 1.3 collective-permute-start.4
  241.5 1.3 collective-permute-start.5
  242.9 3.6 collective-permute-done.5
  248.8 38.4 %scatter_fusion = s32[8,128]{1,0:T(8,128)} fusion(s32[8,128]{1,0:T(8,128)} %broadcast.159, s32[256]{0:T(256)S(1)} %bitcast.151, s32[256]{0:T(256)} %param.16), kind=kCustom, calls=%fused_computation.3 | custom fusion | bytes 5120 | tf_op jit(solution)/shard_map/scatter | solution.py:112
  287.1 6.3 all-to-all-start
  293.6 5.1 all-to-all-done
  298.7 2.4 fusion.19
  301.2 2.2 fusion.22
  303.9 3.2 gather_fusion.1
  308.0 3.4 all-to-all-start.1
  312.4 5.7 all-to-all-done.1
  318.3 1.7 gather_fusion.2
  321.9 16.8 %scatter_fusion.2 = f32[8,128,96]{2,1,0:T(8,128)S(1)} fusion(f32[8,128,96]{2,1,0:T(8,128)S(1)} %broadcast_in_dim.5, s32[256]{0:T(256)S(1)} %bitcast.152, f32[256,96]{1,0:T(8,128)} %copy.100), kind=kCustom, calls=%fused_computation.5 | custom fusion | bytes 296960 | tf_op jit(solution)/shard_map/scatter | solution.py:131
  339.5 4.0 all-to-all-start.2
  343.7 2.4 scatter_fusion.1
  346.1 4.3 all-to-all-done.2
  351.4 6.3 scatter_fusion.3
  357.8 2.7 collective-permute-start.7
  360.5 1.6 fusion.104
  362.1 1.3 collective-permute-start.6
  364.0 1.7 collective-permute-done.6
  365.7 1.8 fusion.6
  367.7 71.6 %reduce-scatter.4.cloned.1.call-done = bf16[96,512]{1,0:T(8,128)(2,1)} async-done(((bf16[1536,512]{1,0:T(8,128)(2,1)}), bf16[96,512]{1,0:T(8,128)(2,1)}) %reduce-scatter.4.cloned.1.call-update) | async-done | bytes 98320 | tf_op jit(solution)/shard_map/reduce_scatter | solution.py:150
  439.3 1.8 multiply_reduce_fusion
  441.2 38.1 %psum.73 = f32[512]{0:T(512)S(1)} all-reduce(f32[512]{0:T(512)S(1)} %get-tuple-element.7), channel_id=1, replica_groups=mesh['seq'=8,'tp'=16] {'tp'}, use_global_device_ids=true, to_apply=%region_17.18 | all-reduce | flops 512 | bytes 4096 | tf_op jit(solution)/shard_map/psum | solution.py:170
  480.6 1.4 collective-permute-start.9
  482.0 1.6 fusion.102
  483.5 1.3 collective-permute-start.8
  485.5 2.9 collective-permute-done.8
  488.4 1.8 fusion.7
  490.3 2.6 fusion.16
  498.7 64.6 %reduce-scatter.6.cloned.1.call-done = bf16[96,512]{1,0:T(8,128)(2,1)} async-done(((bf16[1536,512]{1,0:T(8,128)(2,1)}), bf16[96,512]{1,0:T(8,128)(2,1)}) %reduce-scatter.6.cloned.1.call-update) | async-done | bytes 98320 | tf_op jit(solution)/shard_map/reduce_scatter | solution.py:150
  563.2 1.8 multiply_reduce_fusion.1
  565.1 38.3 %psum.74 = f32[512]{0:T(512)S(1)} all-reduce(f32[512]{0:T(512)S(1)} %get-tuple-element.5), channel_id=1, replica_groups=mesh['seq'=8,'tp'=16] {'tp'}, use_global_device_ids=true, to_apply=%region_20.21 | all-reduce | flops 512 | bytes 4096 | tf_op jit(solution)/shard_map/psum | solution.py:170
  603.4 2.0 fusion.167
  605.4 2.3 fusion.10
  610.3 1.3 collective-permute-start.11
  612.2 1.3 collective-permute-start.10
  614.2 2.9 collective-permute-done.10
  617.1 1.8 fusion.8
  618.9 20.1 %all-gather.1 = f32[16,1,256]{2,1,0:T(1,128)S(1)} all-gather(f32[1,1,256]{2,1,0:T(1,128)S(1)} %bitcast.162), channel_id=2, replica_groups=mesh['seq'=8,'tp'=16] {'tp'}, dimensions={0}, use_global_device_ids=true | all-gather | bytes 17408 | tf_op jit(solution)/shard_map/all_gather | solution.py:127
  639.6 35.1 %all-reduce.3.cloned.1.call-done = (bf16[1,96,3,1536]{3,1,2,0:T(8,128)(2,1)}, bf16[1,96,3,1536]{3,1,2,0:T(8,128)(2,1)}, bf16[1,96,3,1536]{3,1,2,0:T(8,128)(2,1)}) async-done(((bf16[1,96,3,1536]{3,1,2,0:T(8,128)(2,1)}, bf16[1,96,3,1536]{3,1,2,0:T(8,128)(2,1)}, bf16[1,96,3,1536]{3,1,2,0:T(8,128)(2,1)}), (bf16[1,96,3,1536]{3,1,2,0:T(8,128)(2,1)}, bf16[1,96,3,1536]{3,1,2,0:T(8,128)(2,1)}, ...) | async-done | bytes 2654224 | tf_op jit(solution)/shard_map/psum | solution.py:165
  674.7 4.5 maximum_convert_fusion
  679.2 72.7 %reduce-scatter.8.cloned.1.call-done = bf16[96,512]{1,0:T(8,128)(2,1)} async-done(((bf16[1536,512]{1,0:T(8,128)(2,1)}), bf16[96,512]{1,0:T(8,128)(2,1)}) %reduce-scatter.8.cloned.1.call-update) | async-done | bytes 98320 | tf_op jit(solution)/shard_map/reduce_scatter | solution.py:150
  751.9 1.3 fusion.142
  753.2 13.7 %psum.79 = f32[3,96]{1,0:T(4,128)} all-reduce(f32[3,96]{1,0:T(4,128)S(1)} %pad_maximum_fusion.15), channel_id=1, replica_groups=mesh['seq'=8,'tp'=16] {'seq'}, use_global_device_ids=true, to_apply=%region_30.31 | all-reduce | flops 288 | bytes 2304 | tf_op jit(solution)/shard_map/psum | solution.py:176
  767.0 38.1 %psum.75 = f32[512]{0:T(512)S(1)} all-reduce(f32[512]{0:T(512)S(1)} %get-tuple-element.9), channel_id=1, replica_groups=mesh['seq'=8,'tp'=16] {'tp'}, use_global_device_ids=true, to_apply=%region_23.24 | all-reduce | flops 512 | bytes 4096 | tf_op jit(solution)/shard_map/psum | solution.py:170
  805.1 1.8 fusion.139
  (158 shorter events, 30.0 us)
Async XLA Ops:
  7.2 312.9 %copy-start = (f32[367,1536]{1,0:T(8,128)S(1)}, f32[367,1536]{1,0:T(8,128)}, u32[]{:S(2)}) copy-start(f32[367,1536]{1,0:T(8,128)} %param.13) | copy-start | bytes 6764548
  7.2 95.9 %all-gather.6.cloned.1.call-start = ((), (), s32[]{:S(2)}) async-start(), calls=%async_computation.6 | async-start | bytes 2088960 | tf_op jit(solution)/shard_map/all_gather | solution.py:104
  8.7 43.4 %copy-start.22 = (f32[96]{0:T(128)}, f32[96]{0:T(128)S(1)}, u32[]{:S(2)}) copy-start(f32[96]{0:T(128)S(1)} %get-tuple-element.44) | copy-start | bytes 1156
  8.7 138.2 %copy-start.24 = (f32[96]{0:T(128)}, f32[96]{0:T(128)S(1)}, u32[]{:S(2)}) copy-start(f32[96]{0:T(128)S(1)} %get-tuple-element.45) | copy-start | bytes 1156
  52.1 2.6 collective-permute-start
  53.4 5.2 collective-permute-start.1
  59.4 137.7 %all-gather.8.cloned.1.call-start = ((), (), s32[]{:S(2)}) async-start(), calls=%async_computation.7 | async-start | bytes 2088960 | tf_op jit(solution)/shard_map/all_gather | solution.py:104
  62.6 137.4 %copy-start.1 = (bf16[96,3,1536]{2,0,1:T(8,128)(2,1)}, bf16[96,3,1536]{2,0,1:T(8,128)(2,1)S(1)}, u32[]{:S(2)}) copy-start(bf16[96,3,1536]{2,0,1:T(8,128)(2,1)S(1)} %get-tuple-element.21) | copy-start | bytes 2654212
  103.1 2.4 copy-start.5
  103.1 4.6 copy-start.7
  103.1 4.6 copy-start.33
  147.1 2.6 collective-permute-start.2
  148.4 4.9 collective-permute-start.3
  154.1 144.6 %all-gather.10.cloned.1.call-start = ((), (), s32[]{:S(2)}) async-start(), calls=%async_computation.8 | async-start | bytes 2088960 | tf_op jit(solution)/shard_map/all_gather | solution.py:104
  197.1 2.3 copy-start.9
  200.1 47.1 %copy-start.18 = (s32[256,1]{0,1:T(1,128)S(1)}, s32[256,1]{0,1:T(1,128)}, u32[]{:S(2)}) copy-start(s32[256,1]{0,1:T(1,128)} %param.15) | copy-start | bytes 3076
  200.5 92.9 %copy-start.31 = (s32[256]{0:T(256)S(1)}, s32[256]{0:T(256)}, u32[]{:S(2)}) copy-start(s32[256]{0:T(256)} %param.14) | copy-start | bytes 3076
  200.5 93.0 %copy-start.14 = (f32[96,512]{1,0:T(8,128)S(1)}, f32[96,512]{1,0:T(8,128)}, u32[]{:S(2)}) copy-start(f32[96,512]{1,0:T(8,128)} %param.18) | copy-start | bytes 589828
  239.4 61.8 %copy-start.15 = (f32[512]{0:T(512)}, f32[512]{0:T(512)S(1)}, u32[]{:S(2)}) copy-start(f32[512]{0:T(512)S(1)} %get-tuple-element.42) | copy-start | bytes 6148
  240.3 2.6 collective-permute-start.4
  241.5 4.9 collective-permute-start.5
  287.1 11.6 %all-to-all-start = ((s32[8,1,128]{2,1,0:T(1,128)}), s32[8,1,128]{2,1,0:T(1,128)S(1)}, u32[]{:S(2)}, u32[]{:S(2)}) async-start(s32[8,1,128]{2,1,0:T(1,128)} %bitcast.27), calls=%async_computation | async-start | bytes 8192 | tf_op jit(solution)/shard_map/all_to_all | solution.py:114
  293.4 7.7 copy-start.17
  298.7 2.5 copy-start.3
  298.7 4.7 copy-start.11
  303.8 7.6 copy-start.32
  307.1 12.9 %copy-start.30 = (s32[256]{0:T(256)S(1)}, s32[256]{0:T(256)}, u32[]{:S(2)}) copy-start(s32[256]{0:T(256)} %param.17) | copy-start | bytes 3076
  308.0 10.1 %all-to-all-start.1 = ((bf16[8,128,96]{1,2,0:T(8,128)(2,1)}), bf16[8,128,96]{1,2,0:T(8,128)(2,1)S(1)}, u32[]{:S(2)}, u32[]{:S(2)}) async-start(bf16[8,128,96]{1,2,0:T(8,128)(2,1)} %copy.95), calls=%async_computation.1 | async-start | bytes 393216 | tf_op jit(solution)/shard_map/all_to_all | solution.py:116
  339.5 10.8 %all-to-all-start.2 = ((bf16[8,128,96]{1,2,0:T(8,128)(2,1)}), bf16[8,128,96]{1,2,0:T(8,128)(2,1)}, u32[]{:S(2)}, u32[]{:S(2)}) async-start(bf16[8,128,96]{1,2,0:T(8,128)(2,1)} %copy.101), calls=%async_computation.2 | async-start | bytes 393216 | tf_op jit(solution)/shard_map/all_to_all | solution.py:132
  343.5 95.8 %reduce-scatter.4.cloned.1.call-start = ((), (), s32[]{:S(2)}) async-start(), calls=%async_computation.9 | async-start | bytes 1671168 | tf_op jit(solution)/shard_map/reduce_scatter | solution.py:150
  357.8 5.6 copy-start.4
  357.8 5.6 collective-permute-start.7
  362.1 3.6 collective-permute-start.6
  367.5 71.8 %copy-start.16 = (f32[512]{0:T(512)S(1)}, f32[512]{0:T(512)}, u32[]{:S(2)}) copy-start(f32[512]{0:T(512)} %copy-done.15) | copy-start | bytes 6148
  367.5 71.8 %copy-start.26 = (f32[96]{0:T(128)S(1)}, f32[96]{0:T(128)}, u32[]{:S(2)}) copy-start(f32[96]{0:T(128)} %get-tuple-element.43) | copy-start | bytes 1156
  367.5 111.8 %copy-start.21 = (f32[512]{0:T(512)S(1)}, f32[512]{0:T(512)}, u32[]{:S(2)}) copy-start(f32[512]{0:T(512)} %get-tuple-element.41) | copy-start | bytes 6148
  367.5 195.7 %reduce-scatter.6.cloned.1.call-start = ((), (), s32[]{:S(2)}) async-start(), calls=%async_computation.10 | async-start | bytes 1671168 | tf_op jit(solution)/shard_map/reduce_scatter | solution.py:150
  480.5 4.4 copy-start.2
  480.6 4.3 collective-permute-start.9
  483.5 4.9 collective-permute-start.8
  490.2 184.4 %all-reduce.3.cloned.1.call-start = ((), (), s32[]{:S(2)}) async-start(), calls=%async_computation.12 | async-start | bytes 5308416 | tf_op jit(solution)/shard_map/psum | solution.py:165
  490.3 2.6 copy-start.12
  493.5 1.9 copy-start.10
  496.8 66.4 %copy-start.25 = (f32[96]{0:T(128)S(1)}, f32[96]{0:T(128)}, u32[]{:S(2)}) copy-start(f32[96]{0:T(128)} %copy-done.24) | copy-start | bytes 1156
  496.8 106.5 %copy-start.20 = (f32[512]{0:T(512)S(1)}, f32[512]{0:T(512)}, u32[]{:S(2)}) copy-start(f32[512]{0:T(512)} %get-tuple-element.39) | copy-start | bytes 6148
  603.4 4.3 copy-start.34
  609.1 2.5 copy-start.6
  610.1 141.8 %reduce-scatter.8.cloned.1.call-start = ((), (), s32[]{:S(2)}) async-start(), calls=%async_computation.11 | async-start | bytes 1671168 | tf_op jit(solution)/shard_map/reduce_scatter | solution.py:150
  610.3 3.2 collective-permute-start.11
  612.2 4.9 collective-permute-start.10
  614.1 4.8 copy-start.27
  674.7 77.3 %copy-start.8 = (bf16[96,512]{1,0:T(8,128)(2,1)S(1)}, bf16[96,512]{1,0:T(8,128)(2,1)}, u32[]{:S(2)}) copy-start(bf16[96,512]{1,0:T(8,128)(2,1)} %param.10) | copy-start | bytes 294916
  674.7 77.3 %copy-start.23 = (f32[96]{0:T(128)S(1)}, f32[96]{0:T(128)}, u32[]{:S(2)}) copy-start(f32[96]{0:T(128)} %copy-done.22) | copy-start | bytes 1156
  674.7 78.5 %copy-start.28 = (f32[96]{0:T(128)S(1)}, f32[96]{0:T(128)}, u32[]{:S(2)}) copy-start(f32[96]{0:T(128)} %get-tuple-element.6) | copy-start | bytes 1156
  674.7 78.5 %copy-start.29 = (f32[96]{0:T(128)S(1)}, f32[96]{0:T(128)}, u32[]{:S(2)}) copy-start(f32[96]{0:T(128)} %get-tuple-element.4) | copy-start | bytes 1156
  674.7 130.4 %copy-start.13 = (f32[96,512]{1,0:T(8,128)S(1)}, f32[96,512]{1,0:T(8,128)}, u32[]{:S(2)}) copy-start(f32[96,512]{1,0:T(8,128)} %get-tuple-element.14) | copy-start | bytes 589828
  674.7 130.4 %copy-start.19 = (f32[512]{0:T(512)S(1)}, f32[512]{0:T(512)}, u32[]{:S(2)}) copy-start(f32[512]{0:T(512)} %get-tuple-element.37) | copy-start | bytes 6148
Sparse Core Ops, SparseCore 0:
  59.5 43.5 all-gather.5
  154.2 42.8 all-gather.7
  247.3 42.8 all-gather.9
  367.6 71.6 reduce-scatter.3
  490.4 72.8 reduce-scatter.5
  610.2 64.3 all-reduce.2
  677.9 73.9 reduce-scatter.7
